TPU v7x, 512 devices: a whole 4x8x8 slice. The times are simulated.
512 devices in a mesh: mem: 16 (over z, core), head: 8 (over y), span: 4 (over x).
Axes of the slice: x: 4, y: 8, z: 8, core: 2. Of those that a mesh axis runs over, the one named last changes fastest.
Arguments:
- query: bfloat16 [4, 2048, 8, 8, 128], P('span', 'mem', 'head'), may hold values from -6 to 6
- new_keys: bfloat16 [4, 2048, 8, 128], P('span', 'mem', 'head'), may hold values from -6 to 6
- new_values: bfloat16 [4, 2048, 8, 128], P('span', 'mem', 'head'), may hold values from -5 to 5
- memory_keys: bfloat16 [512, 128, 8, 128], P('mem', None, 'head'), may hold values from -5 to 5
- memory_values: bfloat16 [512, 128, 8, 128], P('mem', None, 'head'), may hold values from -5 to 5
- retrieved: int32 [4, 8, 16], P('span', 'head'), may hold values from 0 to 511, as said below
Outputs:
- attended: bfloat16 [4, 2048, 8192], P('span', ('mem', 'head'))
Inputs may be any that keep to these rules, and one draw needn't show every extreme that they name: Each list retrieved[b, h, :] names 16 different units. The units o * 32 to (o + 1) * 32 - 1 appear at most 3 times in one list, and in every list some o has exactly 3.
All inputs are finite; a program needn't handle non-finite values.
Results may differ from a plain program's by a relative error of at most 0.005.
Values may be sent and summed in bfloat16 or wider, within the bound.
A program may use at most 64 MiB of HBM per device.

v0:
```python
import math
import jax
import jax.numpy as jnp
from jax import lax
from jax.sharding import PartitionSpec as P

NEG = -1e30


def shifted(value, axis, steps):
    count = lax.axis_size(axis)
    first, last = (max(0, -steps), min(count, count - steps))
    return lax.ppermute(value, axis, [(source, source + steps) for source in range(first, last)])


def local(query, new_keys, new_values, memory_keys, memory_values, retrieved):
    queries = query[0]
    row_count, head_count, group_size, head_width = queries.shape
    score_scale = 1.0 / math.sqrt(head_width)
    mem_count = lax.axis_size("mem")
    mem_index = lax.axis_index("mem")
    block_index = lax.axis_index("span")
    row_position = mem_index * row_count + jnp.arange(row_count, dtype=jnp.int32)

    def update(carry_state, key_pair, key_mask):
        old_peak, old_total, old_accum = carry_state
        scores = (
            jnp.einsum("rhgd,khd->rhgk", queries, key_pair[0], preferred_element_type=jnp.float32)
            * score_scale
        )
        scores = jnp.where(key_mask, scores, NEG)
        new_peak = jnp.maximum(old_peak, jnp.max(scores, axis=-1))
        weights = jnp.where(key_mask, jnp.exp(scores - new_peak[..., None]), 0.0)
        factor = jnp.exp(old_peak - new_peak)
        new_total = old_total * factor + jnp.sum(weights, axis=-1)
        new_accum = old_accum * factor[..., None] + jnp.einsum(
            "rhgk,khd->rhgd",
            weights.astype(jnp.bfloat16),
            key_pair[1],
            preferred_element_type=jnp.float32,
        )
        return (new_peak, new_total, new_accum)

    def sweep(carry_state, key_pair, first_key, mask_maker):
        key_count = key_pair.shape[1]
        step_size = math.gcd(key_count, 512)

        def advance(step_index, loop_state):
            sub_pair = lax.dynamic_slice_in_dim(key_pair, step_index * step_size, step_size, 1)
            key_position = (
                first_key + step_index * step_size + jnp.arange(step_size, dtype=jnp.int32)
            )
            return update(loop_state, sub_pair, mask_maker(key_position))

        return lax.fori_loop(0, key_count // step_size, advance, carry_state)

    def current_mask(key_position):
        return (key_position[None, :] <= row_position[:, None])[:, None, None, :]

    def prior_mask(key_position):
        return ((key_position[None, :] > row_position[:, None]) & (block_index > 0))[
            :, None, None, :
        ]

    def full_mask(key_position):
        return jnp.ones((1, 1, 1, key_position.shape[0]), bool)

    carry_state = (
        jnp.full((row_count, head_count, group_size), NEG, jnp.float32),
        jnp.zeros((row_count, head_count, group_size), jnp.float32),
        jnp.zeros((row_count, head_count, group_size, head_width), jnp.float32),
    )
    own_pair = jnp.stack([new_keys[0], new_values[0]])
    prior_pair = shifted(own_pair, "span", 1)
    loop_state = carry_state
    first_key = jnp.int32(0)
    loop_state = sweep(
        loop_state, lax.all_gather(own_pair, "mem", axis=1, tiled=True), first_key, current_mask
    )
    carry_state = sweep(
        loop_state, lax.all_gather(prior_pair, "mem", axis=1, tiled=True), first_key, prior_mask
    )
    unit_lists = retrieved[0]
    list_length = unit_lists.shape[1]
    units_dev = memory_keys.shape[0]
    unit_length = memory_keys.shape[1]
    owners = unit_lists // units_dev
    local_units = unit_lists % units_dev
    owned_here = owners == mem_index
    capacity = max(3, 2 * list_length // mem_count)
    ranking = jnp.cumsum(owned_here.astype(jnp.int32), axis=1) - 1
    slot_range = jnp.arange(capacity, dtype=jnp.int32)
    matches = owned_here[:, :, None] & (ranking[:, :, None] == slot_range[None, None, :])
    picked_units = jnp.sum(jnp.where(matches, local_units[:, :, None], 0), axis=1)
    gathered_pair = []
    for source_array in (memory_keys, memory_values):
        per_head = [source_array[picked_units[0], :, 0, :]]
        gathered_pair.append(jnp.stack(per_head, axis=2))
    block_pair = jnp.stack(gathered_pair).reshape(2, capacity * unit_length, head_count, head_width)
    gathered = lax.all_gather(block_pair, "mem", axis=1, tiled=True)
    gathered = gathered.reshape(2, mem_count * capacity, unit_length, head_count, head_width)
    entry_range = jnp.arange(list_length, dtype=jnp.int32)
    earlier = entry_range[None, :] < entry_range[:, None]
    same_owner = owners[:, :, None] == owners[:, None, :]
    owner_rank = jnp.sum((same_owner & earlier[None, :, :]).astype(jnp.int32), axis=2)
    slot_index = owners * capacity + owner_rank
    live_heads = [gathered[:, :, :, 0, :][:, slot_index[0]]]
    live_pair = jnp.stack(live_heads, axis=3).reshape(
        2, list_length * unit_length, head_count, head_width
    )
    carry_state = sweep(carry_state, live_pair, 0, full_mask)
    final_peak, final_total, final_accum = carry_state
    attended = (final_accum / final_total[..., None]).astype(jnp.bfloat16)
    attended = attended.reshape(row_count, head_count * group_size * head_width)
    moved = lax.all_to_all(attended, "head", split_axis=0, concat_axis=1, tiled=True)
    return moved[None]


def solution(mesh):
    return jax.shard_map(
        local,
        mesh=mesh,
        in_specs=(
            P("span", "mem", "head", None, None),
            P("span", "mem", "head", None),
            P("span", "mem", "head", None),
            P("mem", None, "head", None),
            P("mem", None, "head", None),
            P("span", "head", None),
        ),
        out_specs=P("span", ("mem", "head"), None),
        check_vma=False,
    )
```

profile of v0, /device:TPU:1, one launch (start us, length us, event | category | flops | bytes accessed | tf_op | source)
XLA Modules:
  0.0 191.3 jit_solution(4977924991710813457)
XLA Ops:
  8.8 3.9 %collective-permute-start = (bf16[2,128,1,128]{3,1,2,0:T(8,128)(2,1)}, bf16[2,128,1,128]{3,1,2,0:T(8,128)(2,1)S(1)}, u32[]{:S(2)}, u32[]{:S(2)}) collective-permute-start(bf16[2,128,1,128]{3,1,2,0:T(8,128)(2,1)} %copy-done.1), channel_id=1, source_target_pairs={{0,1},{1,2},{2,3},{4,5},{5,6},{6,7},{8,9},{9,10},{10,11},{12,13},{... | collective-permute-start | bytes 196616 | tf_op jit(solution)/shard_map/ppermute | solution.py:13
  12.8 1.6 collective-permute-done
  18.1 1.8 gather_fusion.1
  22.7 34.6 %all-gather.4.cloned.1.call-done = bf16[2,2048,1,128]{3,1,2,0:T(8,128)(2,1)} async-done(((bf16[2,128,1,128]{3,1,2,0:T(8,128)(2,1)}), bf16[2,2048,1,128]{3,1,2,0:T(8,128)(2,1)}) %all-gather.4.cloned.1.call-update) | async-done | bytes 1048592 | tf_op jit(solution)/shard_map/all_gather | solution.py:78
  57.3 18.6 %while.57 = (s32[]{:T(128)}, f32[128,1,8]{0,2,1:T(8,128)S(1)}, f32[128,1,8]{0,2,1:T(8,128)S(1)}, f32[128,1,8,128]{0,3,2,1:T(8,128)}, bf16[2,2048,1,128]{3,1,2,0:...) while((s32[]{:T(128)}, f32[128,1,8]{0,2,1:T(8,128)S(1)}, ...), condition=%wide.region_3.4_spmd.clone, body=%wide.region_0.3_spmd.clone.sunk | while | flops 275716736 | bytes 8197327 | solution.py:55
  57.5 1.4 fusion.89
  58.8 2.4 %fusion.92 = f32[128,1,8,128]{0,3,2,1:T(8,128)} fusion(f32[512,128,8]{1,0,2:T(8,128)S(1)} %get-tuple-element.707, f32[128,8]{0,1:T(8,128)S(1)} %bitcast.263, pred[128,512]{0,1:T(8,128)(4,1)S(1)} %broadcast_compare_fusion.3, f32[128,1,8,128]{0,3,2,1:T(8,128)} %get-tuple-element.724, f32[128,8]{0,1:T(8,128)S(1)} %get-tuple-element.708, ...), kind=kOutput, calls=%fused_computation.61.clone.1 | convolution fusion | flops 137232384 | bytes 3350537 | tf_op jit(solution)/shard_map/while/body/eval_jaxpr/rhgk,khd->rhgd/dot_general | solution.py:36
  63.3 2.6 %fusion.92 = f32[128,1,8,128]{0,3,2,1:T(8,128)} fusion(f32[512,128,8]{1,0,2:T(8,128)S(1)} %get-tuple-element.707, f32[128,8]{0,1:T(8,128)S(1)} %bitcast.263, pred[128,512]{0,1:T(8,128)(4,1)S(1)} %broadcast_compare_fusion.3, f32[128,1,8,128]{0,3,2,1:T(8,128)} %get-tuple-element.724, f32[128,8]{0,1:T(8,128)S(1)} %get-tuple-element.708, ...), kind=kOutput, calls=%fused_computation.61.clone.1 | convolution fusion | flops 137232384 | bytes 3350537 | tf_op jit(solution)/shard_map/while/body/eval_jaxpr/rhgk,khd->rhgd/dot_general | solution.py:36
  68.0 2.6 %fusion.92 = f32[128,1,8,128]{0,3,2,1:T(8,128)} fusion(f32[512,128,8]{1,0,2:T(8,128)S(1)} %get-tuple-element.707, f32[128,8]{0,1:T(8,128)S(1)} %bitcast.263, pred[128,512]{0,1:T(8,128)(4,1)S(1)} %broadcast_compare_fusion.3, f32[128,1,8,128]{0,3,2,1:T(8,128)} %get-tuple-element.724, f32[128,8]{0,1:T(8,128)S(1)} %get-tuple-element.708, ...), kind=kOutput, calls=%fused_computation.61.clone.1 | convolution fusion | flops 137232384 | bytes 3350537 | tf_op jit(solution)/shard_map/while/body/eval_jaxpr/rhgk,khd->rhgd/dot_general | solution.py:36
  72.7 2.6 %fusion.92 = f32[128,1,8,128]{0,3,2,1:T(8,128)} fusion(f32[512,128,8]{1,0,2:T(8,128)S(1)} %get-tuple-element.707, f32[128,8]{0,1:T(8,128)S(1)} %bitcast.263, pred[128,512]{0,1:T(8,128)(4,1)S(1)} %broadcast_compare_fusion.3, f32[128,1,8,128]{0,3,2,1:T(8,128)} %get-tuple-element.724, f32[128,8]{0,1:T(8,128)S(1)} %get-tuple-element.708, ...), kind=kOutput, calls=%fused_computation.61.clone.1 | convolution fusion | flops 137232384 | bytes 3350537 | tf_op jit(solution)/shard_map/while/body/eval_jaxpr/rhgk,khd->rhgd/dot_general | solution.py:36
  75.9 23.7 %all-gather.6.cloned.1.call-done = bf16[2,2048,1,128]{3,1,2,0:T(8,128)(2,1)} async-done(((bf16[2,128,1,128]{3,1,2,0:T(8,128)(2,1)}), bf16[2,2048,1,128]{3,1,2,0:T(8,128)(2,1)}) %all-gather.6.cloned.1.call-update) | async-done | bytes 1048592 | tf_op jit(solution)/shard_map/all_gather | solution.py:81
  99.6 18.8 %while.56 = (s32[]{:T(128)}, f32[128,1,8]{0,2,1:T(8,128)S(1)}, f32[128,1,8]{0,2,1:T(8,128)S(1)}, f32[128,1,8,128]{0,3,2,1:T(8,128)}, pred[]{:T(512)}, /*index=5*...) while((s32[]{:T(128)}, f32[128,1,8]{0,2,1:T(8,128)S(1)}, ...), condition=%wide.region_7.8_spmd.clone, body=%wide.region_4.7_spmd.clone.sunk | while | flops 275648128 | bytes 8197324 | solution.py:55
  101.1 2.6 %fusion.87 = f32[128,1,8,128]{0,3,2,1:T(8,128)} fusion(f32[512,128,8]{1,0,2:T(8,128)S(1)} %get-tuple-element.696, f32[128,8]{0,1:T(8,128)S(1)} %bitcast.261, pred[128,512]{0,1:T(8,128)(4,1)S(1)} %compare_and_fusion.2, f32[128,1,8,128]{0,3,2,1:T(8,128)} %get-tuple-element.761, f32[128,8]{0,1:T(8,128)S(1)} %get-tuple-element.697, ...), kind=kOutput, calls=%fused_computation.32.clone.1 | convolution fusion | flops 137101312 | bytes 3350536 | tf_op jit(solution)/shard_map/while/body/eval_jaxpr/rhgk,khd->rhgd/dot_general | solution.py:36
  105.8 2.6 %fusion.87 = f32[128,1,8,128]{0,3,2,1:T(8,128)} fusion(f32[512,128,8]{1,0,2:T(8,128)S(1)} %get-tuple-element.696, f32[128,8]{0,1:T(8,128)S(1)} %bitcast.261, pred[128,512]{0,1:T(8,128)(4,1)S(1)} %compare_and_fusion.2, f32[128,1,8,128]{0,3,2,1:T(8,128)} %get-tuple-element.761, f32[128,8]{0,1:T(8,128)S(1)} %get-tuple-element.697, ...), kind=kOutput, calls=%fused_computation.32.clone.1 | convolution fusion | flops 137101312 | bytes 3350536 | tf_op jit(solution)/shard_map/while/body/eval_jaxpr/rhgk,khd->rhgd/dot_general | solution.py:36
  110.5 2.6 %fusion.87 = f32[128,1,8,128]{0,3,2,1:T(8,128)} fusion(f32[512,128,8]{1,0,2:T(8,128)S(1)} %get-tuple-element.696, f32[128,8]{0,1:T(8,128)S(1)} %bitcast.261, pred[128,512]{0,1:T(8,128)(4,1)S(1)} %compare_and_fusion.2, f32[128,1,8,128]{0,3,2,1:T(8,128)} %get-tuple-element.761, f32[128,8]{0,1:T(8,128)S(1)} %get-tuple-element.697, ...), kind=kOutput, calls=%fused_computation.32.clone.1 | convolution fusion | flops 137101312 | bytes 3350536 | tf_op jit(solution)/shard_map/while/body/eval_jaxpr/rhgk,khd->rhgd/dot_general | solution.py:36
  115.2 2.6 %fusion.87 = f32[128,1,8,128]{0,3,2,1:T(8,128)} fusion(f32[512,128,8]{1,0,2:T(8,128)S(1)} %get-tuple-element.696, f32[128,8]{0,1:T(8,128)S(1)} %bitcast.261, pred[128,512]{0,1:T(8,128)(4,1)S(1)} %compare_and_fusion.2, f32[128,1,8,128]{0,3,2,1:T(8,128)} %get-tuple-element.761, f32[128,8]{0,1:T(8,128)S(1)} %get-tuple-element.697, ...), kind=kOutput, calls=%fused_computation.32.clone.1 | convolution fusion | flops 137101312 | bytes 3350536 | tf_op jit(solution)/shard_map/while/body/eval_jaxpr/rhgk,khd->rhgd/dot_general | solution.py:36
  118.3 25.6 %all-gather.8.cloned.1.call-done = bf16[2,6144,1,128]{3,1,0,2:T(8,128)(2,1)} async-done(((bf16[2,384,1,128]{3,1,0,2:T(8,128)(2,1)}), bf16[2,6144,1,128]{3,1,0,2:T(8,128)(2,1)}) %all-gather.8.cloned.1.call-update) | async-done | bytes 3145744 | tf_op jit(solution)/shard_map/all_gather | solution.py:100
  143.9 2.6 %gather_fusion.2 = bf16[16,2,128,128]{3,2,1,0:T(8,128)(2,1)S(1)} fusion(bf16[2,48,128,128]{3,2,1,0:T(8,128)(2,1)} %bitcast.269, s32[1024]{0:T(1024)S(1)} %pad_clamp_fusion), kind=kCustom, calls=%fused_computation.2 | custom fusion | bytes 2097216 | tf_op jit(solution)/shard_map/gather | solution.py:107
  147.6 17.0 %while.55 = (s32[]{:T(128)}, f32[128,1,8]{0,2,1:T(8,128)S(1)}, f32[128,1,8]{0,2,1:T(8,128)S(1)}, f32[128,1,8,128]{0,3,2,1:T(8,128)}, bf16[2,2048,1,128]{3,1,2,0:...) while((s32[]{:T(128)}, f32[128,1,8]{0,2,1:T(8,128)S(1)}, ...), condition=%wide.region_14.15_spmd, body=%wide.region_11.14_spmd.sunk | while | flops 272894976 | bytes 7930035 | solution.py:55
  149.0 2.5 %fusion.82 = f32[128,1,8,128]{0,3,2,1:T(8,128)} fusion(f32[512,128,8]{1,0,2:T(8,128)S(1)} %get-tuple-element.684, f32[128,8]{0,1:T(8,128)S(1)} %bitcast.259, f32[128,1,8,128]{0,3,2,1:T(8,128)} %get-tuple-element.798, f32[128,8]{0,1:T(8,128)S(1)} %get-tuple-element.685, bf16[2,2048,1,128]{3,1,2,0:T(8,128)(2,1)} %get-tuple-element.810, s32[]{:T(128)S(6)} %add.337, ...), kind=kOutput, calls=%fused_computation.11.clone.1 | convolution fusion | flops 136052736 | bytes 3285000 | tf_op jit(solution)/shard_map/while/body/eval_jaxpr/rhgk,khd->rhgd/dot_general | solution.py:36
  153.2 2.5 %fusion.82 = f32[128,1,8,128]{0,3,2,1:T(8,128)} fusion(f32[512,128,8]{1,0,2:T(8,128)S(1)} %get-tuple-element.684, f32[128,8]{0,1:T(8,128)S(1)} %bitcast.259, f32[128,1,8,128]{0,3,2,1:T(8,128)} %get-tuple-element.798, f32[128,8]{0,1:T(8,128)S(1)} %get-tuple-element.685, bf16[2,2048,1,128]{3,1,2,0:T(8,128)(2,1)} %get-tuple-element.810, s32[]{:T(128)S(6)} %add.337, ...), kind=kOutput, calls=%fused_computation.11.clone.1 | convolution fusion | flops 136052736 | bytes 3285000 | tf_op jit(solution)/shard_map/while/body/eval_jaxpr/rhgk,khd->rhgd/dot_general | solution.py:36
  157.5 2.5 %fusion.82 = f32[128,1,8,128]{0,3,2,1:T(8,128)} fusion(f32[512,128,8]{1,0,2:T(8,128)S(1)} %get-tuple-element.684, f32[128,8]{0,1:T(8,128)S(1)} %bitcast.259, f32[128,1,8,128]{0,3,2,1:T(8,128)} %get-tuple-element.798, f32[128,8]{0,1:T(8,128)S(1)} %get-tuple-element.685, bf16[2,2048,1,128]{3,1,2,0:T(8,128)(2,1)} %get-tuple-element.810, s32[]{:T(128)S(6)} %add.337, ...), kind=kOutput, calls=%fused_computation.11.clone.1 | convolution fusion | flops 136052736 | bytes 3285000 | tf_op jit(solution)/shard_map/while/body/eval_jaxpr/rhgk,khd->rhgd/dot_general | solution.py:36
  161.7 2.5 %fusion.82 = f32[128,1,8,128]{0,3,2,1:T(8,128)} fusion(f32[512,128,8]{1,0,2:T(8,128)S(1)} %get-tuple-element.684, f32[128,8]{0,1:T(8,128)S(1)} %bitcast.259, f32[128,1,8,128]{0,3,2,1:T(8,128)} %get-tuple-element.798, f32[128,8]{0,1:T(8,128)S(1)} %get-tuple-element.685, bf16[2,2048,1,128]{3,1,2,0:T(8,128)(2,1)} %get-tuple-element.810, s32[]{:T(128)S(6)} %add.337, ...), kind=kOutput, calls=%fused_computation.11.clone.1 | convolution fusion | flops 136052736 | bytes 3285000 | tf_op jit(solution)/shard_map/while/body/eval_jaxpr/rhgk,khd->rhgd/dot_general | solution.py:36
  166.0 17.8 %all_to_all.16 = bf16[8,16,1024]{2,1,0:T(8,128)(2,1)S(1)} all-to-all(bf16[8,16,1024]{2,1,0:T(8,128)(2,1)S(1)} %all_to_all.12), channel_id=1, replica_groups=mesh['mem'=16,'head'=8,'span'=4] {'head'}, dimensions={0} | all-to-all | bytes 524288 | tf_op jit(solution)/shard_map/all_to_all | solution.py:115
  (122 shorter events, 34.1 us)
Async XLA Ops:
  6.5 11.0 %copy-start = (bf16[32,128,1,128]{3,1,2,0:T(8,128)(2,1)S(1)}, bf16[32,128,1,128]{3,1,2,0:T(8,128)(2,1)}, u32[]{:S(2)}) copy-start(bf16[32,128,1,128]{3,1,2,0:T(8,128)(2,1)} %param.15) | copy-start | bytes 3145732
  6.5 50.8 %all-gather.4.cloned.1.call-start = ((), (), s32[]{:S(2)}) async-start(), calls=%async_computation.1 | async-start | bytes 1114112 | tf_op jit(solution)/shard_map/all_gather | solution.py:78
  8.2 0.6 copy-start.1
  8.8 90.8 %all-gather.6.cloned.1.call-start = ((), (), s32[]{:S(2)}) async-start(), calls=%async_computation.2 | async-start | bytes 1114112 | tf_op jit(solution)/shard_map/all_gather | solution.py:81
  8.8 5.6 %collective-permute-start = (bf16[2,128,1,128]{3,1,2,0:T(8,128)(2,1)}, bf16[2,128,1,128]{3,1,2,0:T(8,128)(2,1)S(1)}, u32[]{:S(2)}, u32[]{:S(2)}) collective-permute-start(bf16[2,128,1,128]{3,1,2,0:T(8,128)(2,1)} %copy-done.1), channel_id=1, source_target_pairs={{0,1},{1,2},{2,3},{4,5},{5,6},{6,7},{8,9},{9,10},{10,11},{12,13},{... | collective-permute-start | bytes 196616 | tf_op jit(solution)/shard_map/ppermute | solution.py:13
  14.4 0.6 copy-start.2
  15.1 128.9 %all-gather.8.cloned.1.call-start = ((), (), s32[]{:S(2)}) async-start(), calls=%async_computation.3 | async-start | bytes 3342336 | tf_op jit(solution)/shard_map/all_gather | solution.py:100
Sparse Core Ops, SparseCore 0:
  9.5 47.7 all-gather.3
  59.4 40.0 all-gather.5
  101.7 42.1 all-gather.7
where the time goes:
time: 192 us; the launch traced here: 191 us
  waiting for transfers between devices  85.5 us (45%)
  matrix products  46.6 us (24%)
  blocking collectives  17.8 us (9%)
  between operations  13.2 us (7%)
  local copies, waits for them, and re-layouts  12.1 us (6%)
  other arithmetic  11.3 us (6%)
  starting transfers between devices  4.02 us (2%)
    all_gather x1, waiting for transfers between devices, local(): lax.all_gather(own_pair, 'mem', axis=1, tiled=True)  34.6 us
    dot_general x12, matrix products, update(): jnp.einsum('rhgk,khd->rhgd', weights.astype(jnp.bfloat16), key_pair[1], p...  30.3 us
    all_gather x1, waiting for transfers between devices, local(): gathered = lax.all_gather(block_pair, 'mem', axis=1, tiled=True)  25.6 us
    all_gather x1, waiting for transfers between devices, local(): lax.all_gather(prior_pair, 'mem', axis=1, tiled=True)  23.7 us
    all_to_all x1, blocking collectives, local(): lax.all_to_all(attended, 'head', split_axis=0, concat_axis=1, tiled=True)  17.8 us
    dot_general x12, matrix products, update(): jnp.einsum('rhgd,khd->rhgk', queries, key_pair[0], preferred_element_type...  16.3 us
    reduce_sum x12, other arithmetic, update(): new_total = old_total * factor + jnp.sum(weights, axis=-1)  5.5 us
    ppermute x1, starting transfers between devices, shifted(): lax.ppermute(value, axis, [(source, source + steps) for source in range(f...  3.94 us
  transfers between devices with their start and end apart: 4, of which 4 were waited for; matrix products, arithmetic and copies ran while one was open for 23% of the time, Pallas kernels for 0%

commit v1 on v0

--- a/solution.py
+++ b/solution.py
@@ -5,6 +5,13 @@
 from jax.sharding import PartitionSpec as P
 
 NEG = -1e30
+
+
+def produce_stacks_all_on_mesh(x_in, row_axis):
+    oldest = lax.all_to_all(
+        jnp.stack([x_in] * lax.axis_size(row_axis)), axis_name=row_axis, split_axis=0, concat_axis=0
+    )
+    return jnp.concatenate(oldest, axis=1)
 
 
 def shifted(value, axis, steps):
@@ -97,7 +104,7 @@
         per_head = [source_array[picked_units[0], :, 0, :]]
         gathered_pair.append(jnp.stack(per_head, axis=2))
     block_pair = jnp.stack(gathered_pair).reshape(2, capacity * unit_length, head_count, head_width)
-    gathered = lax.all_gather(block_pair, "mem", axis=1, tiled=True)
+    gathered = produce_stacks_all_on_mesh(block_pair, "mem")
     gathered = gathered.reshape(2, mem_count * capacity, unit_length, head_count, head_width)
     entry_range = jnp.arange(list_length, dtype=jnp.int32)
     earlier = entry_range[None, :] < entry_range[:, None]

time: 192 us -> 184 us (0.958)
  matrix products: 46.6 us -> 28.2 us
  starting transfers between devices: 4.02 us -> 15.4 us
  local copies, waits for them, and re-layouts: 12.1 us -> 18.6 us
  waiting for transfers between devices: 85.5 us -> 79.5 us
  other arithmetic: 11.3 us -> 8.97 us
    all_gather x1 -> x0, waiting for transfers between devices: 25.6 us -> none  [local(): gathered = lax.all_gather(block_pair, 'mem', axis=1, tiled=True)]
    all_gather x1, waiting for transfers between devices: 23.7 us -> 39.4 us  [local(): lax.all_gather(prior_pair, 'mem', axis=1, tiled=True)]
    dot_general x12, matrix products: 30.3 us -> 15.5 us  [update(): jnp.einsum('rhgk,khd->rhgd', weights.astype(jnp.bfloat16), key_pair[1], p...]
    all_to_all x0 -> x1, starting transfers between devices: none -> 11.4 us  [produce_stacks_all_on_mesh(): lax.all_to_all(jnp.stack([x_in] * lax.axis_size(row_axis)), axis_name=row...]
    all_gather x1, waiting for transfers between devices: 34.6 us -> 40.1 us  [local(): lax.all_gather(own_pair, 'mem', axis=1, tiled=True)]
    all_to_all x0 -> x1, local copies, waits for them, and re-layouts: none -> 3.93 us  [produce_stacks_all_on_mesh(): lax.all_to_all(jnp.stack([x_in] * lax.axis_size(row_axis)), axis_name=row...]
    dot_general x12, matrix products: 16.3 us -> 12.7 us  [update(): jnp.einsum('rhgd,khd->rhgk', queries, key_pair[0], preferred_element_type...]
    another operation x0 -> x1, local copies, waits for them, and re-layouts: none -> 2.41 us  [produce_stacks_all_on_mesh(): jnp.stack([x_in] * lax.axis_size(row_axis))]
  transfers between devices with their start and end apart: 4 -> 4, of which waited for: 4 -> 2; matrix products, arithmetic and copies ran while one was open for 23% -> 20% of each run, Pallas kernels for 0% -> 0%
where the time goes in v1:
time: 184 us; the launch traced here: 183 us
  waiting for transfers between devices  79.5 us (43%)
  matrix products  28.2 us (15%)
  local copies, waits for them, and re-layouts  18.6 us (10%)
  blocking collectives  18.2 us (10%)
  starting transfers between devices  15.4 us (8%)
  between operations  13.6 us (7%)
  other arithmetic  8.97 us (5%)
    all_gather x1, waiting for transfers between devices, local(): lax.all_gather(own_pair, 'mem', axis=1, tiled=True)  40.1 us
    all_gather x1, waiting for transfers between devices, local(): lax.all_gather(prior_pair, 'mem', axis=1, tiled=True)  39.4 us
    all_to_all x1, blocking collectives, local(): lax.all_to_all(attended, 'head', split_axis=0, concat_axis=1, tiled=True)  18.2 us
    dot_general x12, matrix products, update(): jnp.einsum('rhgk,khd->rhgd', weights.astype(jnp.bfloat16), key_pair[1], p...  15.5 us
    dot_general x12, matrix products, update(): jnp.einsum('rhgd,khd->rhgk', queries, key_pair[0], preferred_element_type...  12.7 us
    all_to_all x1, starting transfers between devices, produce_stacks_all_on_mesh(): lax.all_to_all(jnp.stack([x_in] * lax.axis_size(row_axis)), axis_name=row...  11.4 us
    reduce_sum x12, other arithmetic, update(): new_total = old_total * factor + jnp.sum(weights, axis=-1)  5.51 us
    gather x2, local copies, waits for them, and re-layouts, local(): live_heads = [gathered[:, :, :, 0, :][:, slot_index[0]]]  4.85 us
  transfers between devices with their start and end apart: 4, of which 2 were waited for; matrix products, arithmetic and copies ran while one was open for 20% of the time, Pallas kernels for 0%

profile of v1, /device:TPU:1, one launch (start us, length us, event | category | flops | bytes accessed | tf_op | source)
XLA Modules:
  0.0 183.3 jit_solution(11340701454112443520)
XLA Ops:
  8.8 3.9 %collective-permute-start = (bf16[2,128,1,128]{3,1,2,0:T(8,128)(2,1)}, bf16[2,128,1,128]{3,1,2,0:T(8,128)(2,1)S(1)}, u32[]{:S(2)}, u32[]{:S(2)}) collective-permute-start(bf16[2,128,1,128]{3,1,2,0:T(8,128)(2,1)} %copy-done.2), channel_id=1, source_target_pairs={{0,1},{1,2},{2,3},{4,5},{5,6},{6,7},{8,9},{9,10},{10,11},{12,13},{... | collective-permute-start | bytes 196616 | tf_op jit(solution)/shard_map/ppermute | solution.py:20
  15.8 1.8 gather_fusion
  17.6 2.4 %stack.17 = bf16[16,2,384,1,128]{4,2,1,3,0:T(8,128)(2,1)} broadcast(bf16[2,384,128]{2,1,0:T(8,128)(2,1)S(1)} %maximum_bitcast_fusion), dimensions={1,2,4} | broadcast | bytes 3342336 | tf_op jit(solution)/shard_map/stack | solution.py:12
  20.0 11.4 %all-to-all-start = ((bf16[16,2,384,1,128]{4,2,1,3,0:T(8,128)(2,1)}), bf16[16,2,384,1,128]{4,2,1,3,0:T(8,128)(2,1)}, u32[]{:S(2)}, u32[]{:S(2)}) async-start(bf16[16,2,384,1,128]{4,2,1,3,0:T(8,128)(2,1)} %stack.17), calls=%async_computation | async-start | bytes 6291456 | tf_op jit(solution)/shard_map/all_to_all | solution.py:11
  32.6 40.1 %all-gather.3.cloned.1.call-done = bf16[2,2048,1,128]{3,1,2,0:T(8,128)(2,1)} async-done(((bf16[2,128,1,128]{3,1,2,0:T(8,128)(2,1)}), bf16[2,2048,1,128]{3,1,2,0:T(8,128)(2,1)}) %all-gather.3.cloned.1.call-update) | async-done | bytes 1048592 | tf_op jit(solution)/shard_map/all_gather | solution.py:85
  72.8 15.0 %while.57 = (s32[]{:T(128)}, f32[128,1,8]{0,2,1:T(8,128)S(1)}, f32[128,1,8]{0,2,1:T(8,128)S(1)}, f32[128,1,8,128]{0,3,2,1:T(8,128)S(1)}, bf16[2,2048,1,128]{3,1,...) while((s32[]{:T(128)}, f32[128,1,8]{0,2,1:T(8,128)S(1)}, ...), condition=%wide.region_3.4_spmd.clone, body=%wide.region_0.3_spmd.clone.sunk | while | flops 275716736 | bytes 8197335 | solution.py:62
  74.8 1.6 fusion.92
  76.7 1.4 fusion.89
  78.6 1.6 fusion.92
  80.4 1.4 fusion.89
  82.3 1.6 fusion.92
  84.2 1.4 fusion.89
  86.1 1.6 fusion.92
  87.8 39.4 %all-gather.5.cloned.1.call-done = bf16[2,2048,1,128]{3,1,2,0:T(8,128)(2,1)} async-done(((bf16[2,128,1,128]{3,1,2,0:T(8,128)(2,1)}), bf16[2,2048,1,128]{3,1,2,0:T(8,128)(2,1)}) %all-gather.5.cloned.1.call-update) | async-done | bytes 1048592 | tf_op jit(solution)/shard_map/all_gather | solution.py:88
  127.1 15.0 %while.56 = (s32[]{:T(128)}, f32[128,1,8]{0,2,1:T(8,128)S(1)}, f32[128,1,8]{0,2,1:T(8,128)S(1)}, f32[128,1,8,128]{0,3,2,1:T(8,128)S(1)}, pred[]{:T(512)}, /*inde...) while((s32[]{:T(128)}, f32[128,1,8]{0,2,1:T(8,128)S(1)}, ...), condition=%wide.region_7.8_spmd.clone, body=%wide.region_4.7_spmd.clone.sunk | while | flops 275648128 | bytes 8197324 | solution.py:62
  127.3 1.4 fusion.84
  129.2 1.6 fusion.87
  133.0 1.6 fusion.87
  136.7 1.6 fusion.87
  140.5 1.6 fusion.87
  142.2 3.9 %copy.85 = bf16[16,2,384,1,128]{4,2,0,1,3:T(8,128)(2,1)} copy(bf16[16,2,384,1,128]{4,2,1,3,0:T(8,128)(2,1)} %all-to-all-done) | data formatting | bytes 6291456 | tf_op jit(solution)/shard_map/all_to_all | solution.py:11
  146.1 3.6 %gather_fusion.2 = bf16[16,2,128,128]{3,2,1,0:T(8,128)(2,1)} fusion(bf16[2,48,128,128]{3,2,1,0:T(8,128)(2,1)} %bitcast.261, s32[1024]{0:T(1024)S(1)} %pad_clamp_fusion), kind=kCustom, calls=%fused_computation.2 | custom fusion | bytes 2097216 | tf_op jit(solution)/shard_map/gather | solution.py:114
  151.0 6.0 %while.55 = (s32[]{:T(128)}, f32[128,1,8]{0,2,1:T(8,128)S(1)}, f32[128,1,8]{0,2,1:T(8,128)S(1)}, f32[128,1,8,128]{0,3,2,1:T(8,128)S(1)}, bf16[2,2048,1,128]{3,1,...) while((s32[]{:T(128)}, f32[128,1,8]{0,2,1:T(8,128)S(1)}, ...), condition=%wide.region_14.15_spmd, body=%wide.region_11.14_spmd.sunk | while | flops 272894976 | bytes 7930035 | solution.py:62
  157.3 18.2 %all_to_all.21 = bf16[8,16,1024]{2,1,0:T(8,128)(2,1)S(1)} all-to-all(bf16[8,16,1024]{2,1,0:T(8,128)(2,1)S(1)} %all_to_all.16), channel_id=1, replica_groups=mesh['mem'=16,'head'=8,'span'=4] {'head'}, dimensions={0} | all-to-all | bytes 524288 | tf_op jit(solution)/shard_map/all_to_all | solution.py:122
  (127 shorter events, 25.6 us)
Async XLA Ops:
  6.5 8.6 %copy-start = (bf16[32,128,1,128]{3,1,2,0:T(8,128)(2,1)S(1)}, bf16[32,128,1,128]{3,1,2,0:T(8,128)(2,1)}, u32[]{:S(2)}) copy-start(bf16[32,128,1,128]{3,1,2,0:T(8,128)(2,1)} %param.16) | copy-start | bytes 3145732
  6.5 66.2 %all-gather.3.cloned.1.call-start = ((), (), s32[]{:S(2)}) async-start(), calls=%async_computation.2 | async-start | bytes 1114112 | tf_op jit(solution)/shard_map/all_gather | solution.py:85
  8.2 0.6 copy-start.2
  8.8 23.2 %collective-permute-start = (bf16[2,128,1,128]{3,1,2,0:T(8,128)(2,1)}, bf16[2,128,1,128]{3,1,2,0:T(8,128)(2,1)S(1)}, u32[]{:S(2)}, u32[]{:S(2)}) collective-permute-start(bf16[2,128,1,128]{3,1,2,0:T(8,128)(2,1)} %copy-done.2), channel_id=1, source_target_pairs={{0,1},{1,2},{2,3},{4,5},{5,6},{6,7},{8,9},{9,10},{10,11},{12,13},{... | collective-permute-start | bytes 196616 | tf_op jit(solution)/shard_map/ppermute | solution.py:20
  20.0 11.5 %copy-start.4 = (s32[1,1,16]{2,1,0:T(1,128)S(1)}, s32[1,1,16]{2,1,0:T(1,128)}, u32[]{:S(2)}) copy-start(s32[1,1,16]{2,1,0:T(1,128)} %param.17) | copy-start | bytes 196
  20.0 11.8 %copy-start.1 = (bf16[1,128,1,8,128]{4,3,2,1,0:T(8,128)(2,1)S(1)}, bf16[1,128,1,8,128]{4,3,2,1,0:T(8,128)(2,1)}, u32[]{:S(2)}) copy-start(bf16[1,128,1,8,128]{4,3,2,1,0:T(8,128)(2,1)} %param.12) | copy-start | bytes 786436
  20.0 122.2 %all-to-all-start = ((bf16[16,2,384,1,128]{4,2,1,3,0:T(8,128)(2,1)}), bf16[16,2,384,1,128]{4,2,1,3,0:T(8,128)(2,1)}, u32[]{:S(2)}, u32[]{:S(2)}) async-start(bf16[16,2,384,1,128]{4,2,1,3,0:T(8,128)(2,1)} %stack.17), calls=%async_computation | async-start | bytes 6291456 | tf_op jit(solution)/shard_map/all_to_all | solution.py:11
  31.4 95.7 %all-gather.5.cloned.1.call-start = ((), (), s32[]{:S(2)}) async-start(), calls=%async_computation.3 | async-start | bytes 1114112 | tf_op jit(solution)/shard_map/all_gather | solution.py:88
  32.0 0.6 copy-start.3
Sparse Core Ops, SparseCore 0:
  9.5 63.2 all-gather.2
  74.9 52.1 all-gather.4
